TPU v7x, 256 devices: a whole 4x4x8 slice. The times are simulated.
256 devices in a mesh: row: 16 (over z, y_lo), col: 16 (over x, y_hi, core).
Axes of the slice: x: 4, y: 4 (y_hi: 2, y_lo: 2; y = y_hi * 2 + y_lo), z: 8, core: 2. Of those that a mesh axis runs over, the one named last changes fastest.
Arguments:
- raw: int32 [32768, 4096], P('col', 'row'), may hold values from -128 to 127
- taps: int32 [16, 128], replicated, may hold values from -256 to 256
Outputs:
- visibility: bfloat16 [32, 4096, 2, 4096], P(None, 'row', None, 'col')
All inputs are finite; a program needn't handle non-finite values.
Results may differ from a plain program's by a relative error of at most 0.0056.
Values may be sent and summed in bfloat16 or wider, within the bound.
A program may use at most 128 MiB of HBM per device.

v0:
```python
import math
import jax
import jax.numpy as jnp
from jax import lax
from jax.sharding import PartitionSpec as P

CHANNELS = 32
TRANSFORM = 128
TAPS = 16
SPECTRA_DEV = 16
BLOCKS = 2


def from_behind(block, axis, distance):
    devices = range(lax.axis_size(axis))
    route = [(i - distance, i) for i in devices if i - distance in devices]
    return lax.ppermute(block, axis, route)


def swap_block(block):
    size = lax.axis_size("row")
    route = [(i * size + j, j * size + i) for i in range(size) for j in range(size)]
    return lax.ppermute(block, ("row", "col"), route)


def dft_table():
    sample = jnp.arange(TRANSFORM, dtype=jnp.int32)[:, None]
    channel = jnp.arange(1, CHANNELS + 1, dtype=jnp.int32)[None, :]
    phase = (sample * channel % TRANSFORM).astype(jnp.float32) * (2.0 * math.pi / TRANSFORM)
    return jnp.concatenate([jnp.cos(phase), -jnp.sin(phase)], axis=1)


def channelize(extended, taps, count):
    coeffs = taps.astype(jnp.float32)
    weighted = jnp.zeros((count, TRANSFORM, extended.shape[2]), jnp.float32)
    for offset in range(TAPS):
        start = TAPS - 1 - offset
        weighted = weighted + coeffs[offset][None, :, None] * extended[
            start : start + count
        ].astype(jnp.float32)
    scale = 1.0 / (8192.0 * math.sqrt(TAPS * TRANSFORM))
    spectra = (
        jnp.einsum("sni,nk->ksi", weighted, dft_table(), precision=lax.Precision.HIGHEST) * scale
    )
    return spectra.reshape(2, CHANNELS, count, extended.shape[2]).astype(jnp.bfloat16)


def correlate(row_block, column_block):
    spectra_all = row_block.shape[2]
    width = spectra_all // BLOCKS
    total = None
    for block in range(BLOCKS):
        left = jnp.concatenate(
            [
                row_block[0, :, block * width : (block + 1) * width],
                row_block[1, :, block * width : (block + 1) * width],
            ],
            axis=1,
        )
        real_part = column_block[0, :, block * width : (block + 1) * width]
        imag_part = column_block[1, :, block * width : (block + 1) * width]
        right = jnp.concatenate(
            [
                jnp.concatenate([real_part, imag_part], axis=1),
                jnp.concatenate([-imag_part, real_part], axis=1),
            ],
            axis=2,
        )
        term = lax.dot_general(
            left, right, (((1,), (1,)), ((0,), (0,))), preferred_element_type=jnp.float32
        )
        if block == 0:
            total = term
        else:
            summed = total + term
            total = summed
    result = (total * (1.0 / spectra_all)).astype(jnp.bfloat16)
    return result.reshape(CHANNELS, row_block.shape[3], 2, column_block.shape[3])


def body(raw, taps):
    frames = raw.astype(jnp.bfloat16).reshape(SPECTRA_DEV, TRANSFORM, raw.shape[1])
    rim_frames = frames[SPECTRA_DEV - (TAPS - 1) :]
    earlier = from_behind(rim_frames, "col", 1)
    extended = jnp.concatenate([earlier, frames], axis=0)
    pieces = channelize(extended, taps, SPECTRA_DEV)
    swapped = swap_block(pieces)
    row_block = lax.all_gather(pieces, "col", axis=2, tiled=True)
    column_block = lax.all_gather(swapped, "row", axis=2, tiled=True)
    return correlate(row_block, column_block)


def solution(mesh):
    placed = (P("col", "row"), P())
    return jax.shard_map(
        body, mesh=mesh, in_specs=placed, out_specs=P(None, "row", None, "col"), check_vma=False
    )
```

profile of v0, /device:TPU:1, one launch (start us, length us, event | category | flops | bytes accessed | tf_op | source)
XLA Modules:
  0.0 380.7 jit_solution(359038543877682941)
XLA Ops:
  6.5 0.0 copy-start.5
  6.5 0.0 all-gather.3.cloned.1.call-start
  6.5 1.8 convert_element_type.70
  8.3 0.1 slice.166
  8.4 6.2 %collective-permute-start = (bf16[15,128,256]{2,1,0:T(8,128)(2,1)S(1)}, bf16[15,128,256]{2,1,0:T(8,128)(2,1)S(1)}, u32[]{:S(2)}, u32[]{:S(2)}) collective-permute-start(bf16[15,128,256]{2,1,0:T(8,128)(2,1)S(1)} %bitcast.61), channel_id=1, source_target_pairs={{0,1},{1,2},{2,3},{3,4},{4,5},{5,6},{6,7},{7,8},{8,9},{9,10},{10,1... | collective-permute-start | bytes 2949128 | tf_op jit(solution)/shard_map/ppermute | solution.py:17
  14.6 0.0 copy-done.5
  14.7 0.2 fusion.128
  14.8 10.8 %collective-permute-done = bf16[15,128,256]{2,1,0:T(8,128)(2,1)S(1)} collective-permute-done((bf16[15,128,256]{2,1,0:T(8,128)(2,1)S(1)}, bf16[15,128,256]{2,1,0:T(8,128)(2,1)S(1)}, u32[]{:S(2)}, u32[]{:S(2)}) %collective-permute-start) | collective-permute-done | bytes 983072 | tf_op jit(solution)/shard_map/ppermute | solution.py:17
  25.6 6.0 %fusion.72 = bf16[64,16,256]{2,0,1:T(8,128)(2,1)} fusion(bf16[16,128,256]{2,1,0:T(8,128)(2,1)S(1)} %bitcast.54, bf16[15,128,256]{2,1,0:T(8,128)(2,1)S(1)} %collective-permute-done, f32[128]{0:T(128)S(1)} %get-tuple-element.16, f32[128]{0:T(128)S(1)} %get-tuple-element.17, f32[128]{0:T(128)S(1)} %get-tuple-element.18, f32[128]{0:T(128)S(1)} %get-tuple-element.19, ...), kind=kOutput, calls=%fused_computation.103 | convolution fusion | flops 451420160 | bytes 2596864 | tf_op jit(solution)/shard_map/sni,nk->ksi/dot_general | solution.py:43
  31.6 0.0 all-gather.3.cloned.1.call-update
  31.6 0.0 all-gather.5.cloned.1.call-start
  31.7 1.3 copy.7
  33.0 1.9 collective-permute-start.1
  34.9 8.7 %collective-permute-done.1 = bf16[2,32,16,256]{3,2,1,0:T(8,128)(2,1)S(1)} collective-permute-done((bf16[2,32,16,256]{3,2,1,0:T(8,128)(2,1)S(1)}, bf16[2,32,16,256]{3,2,1,0:T(8,128)(2,1)S(1)}, u32[]{:S(2)}, u32[]{:S(2)}) %collective-permute-start.1) | collective-permute-done | bytes 524320 | tf_op jit(solution)/shard_map/ppermute | solution.py:23
  43.7 0.0 copy-start.4
  43.7 0.8 copy-done.4
  44.5 0.0 all-gather.5.cloned.1.call-update
  44.5 101.8 %all-gather.3.cloned.1.call-done = bf16[2,32,256,256]{3,1,0,2:T(8,128)(2,1)} async-done(((bf16[2,32,16,256]{3,1,0,2:T(8,128)(2,1)}), bf16[2,32,256,256]{3,1,0,2:T(8,128)(2,1)}) %all-gather.3.cloned.1.call-update) | async-done | bytes 8388624 | tf_op jit(solution)/shard_map/all_gather | solution.py:88
  146.3 5.8 %fusion.135 = (bf16[1,32,128,256]{3,1,0,2:T(8,128)(2,1)}, bf16[1,32,128,256]{3,1,0,2:T(8,128)(2,1)}, bf16[1,32,128,256]{3,1,0,2:T(8,128)(2,1)}, bf16[1,32,128,256]{3,1,0,2:T(8,128)(2,1)S(1)}) fusion(bf16[2,32,256,256]{3,1,0,2:T(8,128)(2,1)} %all-gather.3.cloned.1.call-done), kind=kLoop, calls=%fused_computation.173 | loop fusion | bytes 16777216 | tf_op jit(solution)/shard_map/slice | solution.py:55
  152.1 4.5 %copy.12 = bf16[1,32,128,256]{2,3,1,0:T(8,128)(2,1)} copy(bf16[1,32,128,256]{3,1,0,2:T(8,128)(2,1)} %get-tuple-element.5) | data formatting | bytes 4194304
  156.7 4.6 %copy.11 = bf16[1,32,128,256]{2,3,1,0:T(8,128)(2,1)} copy(bf16[1,32,128,256]{3,1,0,2:T(8,128)(2,1)} %get-tuple-element.6) | data formatting | bytes 4194304
  161.2 4.5 %copy.10 = bf16[1,32,128,256]{2,3,1,0:T(8,128)(2,1)} copy(bf16[1,32,128,256]{3,1,0,2:T(8,128)(2,1)} %get-tuple-element.7) | data formatting | bytes 4194304
  165.8 3.1 copy.13
  168.9 159.2 %all-gather.5.cloned.1.call-done = bf16[2,32,256,256]{3,2,1,0:T(8,128)(2,1)} async-done(((bf16[2,32,16,256]{3,2,1,0:T(8,128)(2,1)}), bf16[2,32,256,256]{3,2,1,0:T(8,128)(2,1)}) %all-gather.5.cloned.1.call-update) | async-done | bytes 8388624 | tf_op jit(solution)/shard_map/all_gather | solution.py:89
  328.1 0.0 copy-start
  328.1 4.0 %fusion.134 = (bf16[32,128,256]{2,1,0:T(8,128)(2,1)}, bf16[32,128,256]{2,1,0:T(8,128)(2,1)S(1)}) fusion(bf16[2,32,256,256]{3,2,1,0:T(8,128)(2,1)} %all-gather.5.cloned.1.call-done), kind=kLoop, calls=%fused_computation.172 | loop fusion | flops 2097152 | bytes 8388608 | tf_op jit(solution)/shard_map/neg | solution.py:65
  332.1 1.4 copy-done
  333.5 0.0 copy-start.2
  333.5 0.0 copy-start.3
  333.5 4.2 %slice_bitcast_fusion = (bf16[32,128,256]{2,1,0:T(8,128)(2,1)}, bf16[32,128,256]{2,1,0:T(8,128)(2,1)}, bf16[32,128,256]{2,1,0:T(8,128)(2,1)}, bf16[32,128,256]{2,1,0:T(8,128)(2,1)}) fusion(bf16[2,32,256,256]{3,2,1,0:T(8,128)(2,1)S(1)} %copy-done), kind=kLoop, calls=%fused_computation.50 | loop fusion | bytes 16777216 | tf_op jit(solution)/shard_map/squeeze | solution.py:61
  337.7 0.0 copy-done.2
  337.7 0.8 copy-done.3
  338.5 0.0 copy-start.1
  338.5 9.2 %fusion = f32[32,256,512]{2,1,0:T(8,128)} fusion(bf16[32,128,256]{2,1,0:T(8,128)(2,1)} %get-tuple-element.12, bf16[32,128,256]{2,1,0:T(8,128)(2,1)S(1)} %get-tuple-element.14, bf16[32,128,256]{2,1,0:T(8,128)(2,1)} %get-tuple-element.11, bf16[32,128,256]{1,2,0:T(8,128)(2,1)S(1)} %bitcast.57, bf16[32,128,256]{1,2,0:T(8,128)(2,1)S(1)} %bitcast.58), kind=kOutput, calls=%fused_computation.1 | convolution fusion | flops 2189426688 | bytes 27262976 | tf_op jit(solution)/shard_map/dot_general | solution.py:69
  347.8 0.0 copy-done.1
  347.8 13.7 %multiply_convert_fusion = bf16[32,256,512]{2,1,0:T(8,128)(2,1)} fusion(f32[32,256,512]{2,1,0:T(8,128)} %fusion, bf16[32,128,256]{2,1,0:T(8,128)(2,1)} %get-tuple-element.10, bf16[32,128,256]{2,1,0:T(8,128)(2,1)} %get-tuple-element.13, bf16[32,128,256]{2,1,0:T(8,128)(2,1)} %get-tuple-element.9, bf16[32,128,256]{1,2,0:T(8,128)(2,1)} %bitcast.56, ...), kind=kOutput, calls=%fused_computation | convolution fusion | flops 2202009600 | bytes 35651584 | tf_op jit(solution)/shard_map/dot_general | solution.py:69
  361.4 12.5 %reshape.30 = bf16[32,256,2,256]{3,2,1,0:T(2,128)(2,1)} reshape(bf16[32,256,512]{2,1,0:T(8,128)(2,1)} %multiply_convert_fusion) | data formatting | bytes 16777216 | tf_op jit(solution)/shard_map/reshape | solution.py:78
  (3 shorter events, 0.0 us)
Async XLA Ops:
  6.5 8.1 %copy-start.5 = (s32[16,128]{1,0:T(8,128)S(1)}, s32[16,128]{1,0:T(8,128)}, u32[]{:S(2)}) copy-start(s32[16,128]{1,0:T(8,128)} %param.3) | copy-start | bytes 24580
  6.5 139.8 %all-gather.3.cloned.1.call-start = ((), (), s32[]{:S(2)}) async-start(), calls=%async_computation | async-start | bytes 8912896 | tf_op jit(solution)/shard_map/all_gather | solution.py:88
  8.4 17.2 %collective-permute-start = (bf16[15,128,256]{2,1,0:T(8,128)(2,1)S(1)}, bf16[15,128,256]{2,1,0:T(8,128)(2,1)S(1)}, u32[]{:S(2)}, u32[]{:S(2)}) collective-permute-start(bf16[15,128,256]{2,1,0:T(8,128)(2,1)S(1)} %bitcast.61), channel_id=1, source_target_pairs={{0,1},{1,2},{2,3},{3,4},{4,5},{5,6},{6,7},{7,8},{8,9},{9,10},{10,1... | collective-permute-start | bytes 2949128 | tf_op jit(solution)/shard_map/ppermute | solution.py:17
  31.6 296.5 %all-gather.5.cloned.1.call-start = ((), (), s32[]{:S(2)}) async-start(), calls=%async_computation.1 | async-start | bytes 8912896 | tf_op jit(solution)/shard_map/all_gather | solution.py:89
  33.0 10.7 %collective-permute-start.1 = (bf16[2,32,16,256]{3,2,1,0:T(8,128)(2,1)S(1)}, bf16[2,32,16,256]{3,2,1,0:T(8,128)(2,1)S(1)}, u32[]{:S(2)}, u32[]{:S(2)}) collective-permute-start(bf16[2,32,16,256]{3,2,1,0:T(8,128)(2,1)S(1)} %copy.7), channel_id=1, source_target_pairs={{0,0},{1,16},{2,32},{3,48},{4,64},{5,80},{6,96},{7,112},{8,128},{9... | collective-permute-start | bytes 1572872 | tf_op jit(solution)/shard_map/ppermute | solution.py:23
  43.7 0.8 copy-start.4
  328.1 5.4 %copy-start = (bf16[2,32,256,256]{3,2,1,0:T(8,128)(2,1)S(1)}, bf16[2,32,256,256]{3,2,1,0:T(8,128)(2,1)}, u32[]{:S(2)}) copy-start(bf16[2,32,256,256]{3,2,1,0:T(8,128)(2,1)} %all-gather.5.cloned.1.call-done) | copy-start | bytes 25165828
  333.5 4.2 %copy-start.2 = (bf16[1,32,128,256]{2,3,1,0:T(8,128)(2,1)S(1)}, bf16[1,32,128,256]{2,3,1,0:T(8,128)(2,1)}, u32[]{:S(2)}) copy-start(bf16[1,32,128,256]{2,3,1,0:T(8,128)(2,1)} %copy.11) | copy-start | bytes 6291460
  333.5 5.0 %copy-start.3 = (bf16[1,32,128,256]{2,3,1,0:T(8,128)(2,1)S(1)}, bf16[1,32,128,256]{2,3,1,0:T(8,128)(2,1)}, u32[]{:S(2)}) copy-start(bf16[1,32,128,256]{2,3,1,0:T(8,128)(2,1)} %copy.10) | copy-start | bytes 6291460
  338.5 9.2 %copy-start.1 = (bf16[1,32,128,256]{2,3,1,0:T(8,128)(2,1)S(1)}, bf16[1,32,128,256]{2,3,1,0:T(8,128)(2,1)}, u32[]{:S(2)}) copy-start(bf16[1,32,128,256]{2,3,1,0:T(8,128)(2,1)} %copy.12) | copy-start | bytes 6291460
Sparse Core Ops, SparseCore 0:
  31.7 114.5 all-gather.2
  148.1 179.9 all-gather.4
where the time goes:
time: 381 us
  waiting for transfers between devices  281 us (74%)
  local copies, waits for them, and re-layouts  43.7 us (11%)
  matrix products  28.9 us (8%)
  between operations  13.5 us (4%)
  starting transfers between devices  8.18 us (2%)
  other arithmetic  5.91 us (2%)
    all_gather x1, waiting for transfers between devices, body(): column_block = lax.all_gather(swapped, 'row', axis=2, tiled=True)  159 us
    all_gather x1, waiting for transfers between devices, body(): row_block = lax.all_gather(pieces, 'col', axis=2, tiled=True)  102 us
    dot_general x2, matrix products, correlate(): lax.dot_general(left, right, (((1,), (1,)), ((0,), (0,))), preferred_elem...  22.9 us
    unnamed x16, local copies, waits for them, and re-layouts  19.8 us
    reshape x1, local copies, waits for them, and re-layouts, correlate(): result.reshape(CHANNELS, row_block.shape[3], 2, column_block.shape[3])  12.5 us
    ppermute x1, waiting for transfers between devices, from_behind(): return lax.ppermute(block, axis, route)  10.8 us
    ppermute x1, waiting for transfers between devices, swap_block(): return lax.ppermute(block, ('row', 'col'), route)  8.74 us
  transfers between devices with their start and end apart: 4, of which 4 were waited for; matrix products, arithmetic and copies ran while one was open for 6% of the time, Pallas kernels for 0%

commit v1 on v0

--- a/solution.py
+++ b/solution.py
@@ -86,7 +86,9 @@
     pieces = channelize(extended, taps, SPECTRA_DEV)
     swapped = swap_block(pieces)
     row_block = lax.all_gather(pieces, "col", axis=2, tiled=True)
-    column_block = lax.all_gather(swapped, "row", axis=2, tiled=True)
+    column_block = jnp.concatenate(
+        lax.all_to_all(jnp.stack([swapped] * lax.axis_size("row")), "row", 0, 0), axis=2
+    )
     return correlate(row_block, column_block)
 
 

time: 381 us -> 351 us (0.921)
  waiting for transfers between devices: 281 us -> 189 us
  starting transfers between devices: 8.18 us -> 57.8 us
  local copies, waits for them, and re-layouts: 43.7 us -> 54.1 us
    all_gather x1 -> x0, waiting for transfers between devices: 159 us -> none  [body(): column_block = lax.all_gather(swapped, 'row', axis=2, tiled=True)]
    all_to_all x0 -> x1, waiting for transfers between devices: none -> 118 us  [body(): lax.all_to_all(jnp.stack([swapped] * lax.axis_size('row')), 'row', 0, 0)]
    all_gather x1, waiting for transfers between devices: 102 us -> 51 us  [body(): row_block = lax.all_gather(pieces, 'col', axis=2, tiled=True)]
    all_to_all x0 -> x1, starting transfers between devices: none -> 49.7 us  [body(): lax.all_to_all(jnp.stack([swapped] * lax.axis_size('row')), 'row', 0, 0)]
    reshape x0 -> x1, local copies, waits for them, and re-layouts: none -> 8.01 us  [body(): jnp.concatenate(lax.all_to_all(jnp.stack([swapped] * lax.axis_size('row')...]
    another operation x0 -> x1, local copies, waits for them, and re-layouts: none -> 4.35 us  [body(): jnp.stack([swapped] * lax.axis_size('row'))]
  transfers between devices with their start and end apart: 4 -> 4, of which waited for: 4 -> 4; matrix products, arithmetic and copies ran while one was open for 6% -> 8% of each run, Pallas kernels for 0% -> 0%
where the time goes in v1:
time: 351 us; the launch traced here: 348 us
  waiting for transfers between devices  189 us (54%)
  starting transfers between devices  57.8 us (16%)
  local copies, waits for them, and re-layouts  54.1 us (15%)
  matrix products  28.1 us (8%)
  between operations  13.5 us (4%)
  other arithmetic  5.91 us (2%)
    all_to_all x1, waiting for transfers between devices, body(): lax.all_to_all(jnp.stack([swapped] * lax.axis_size('row')), 'row', 0, 0)  118 us
    all_gather x1, waiting for transfers between devices, body(): row_block = lax.all_gather(pieces, 'col', axis=2, tiled=True)  51 us
    all_to_all x1, starting transfers between devices, body(): lax.all_to_all(jnp.stack([swapped] * lax.axis_size('row')), 'row', 0, 0)  49.7 us
    dot_general x2, matrix products, correlate(): lax.dot_general(left, right, (((1,), (1,)), ((0,), (0,))), preferred_elem...  22.9 us
    unnamed x16, local copies, waits for them, and re-layouts  18.9 us
    reshape x1, local copies, waits for them, and re-layouts, correlate(): result.reshape(CHANNELS, row_block.shape[3], 2, column_block.shape[3])  12.5 us
    ppermute x1, waiting for transfers between devices, from_behind(): return lax.ppermute(block, axis, route)  10.8 us
    ppermute x1, waiting for transfers between devices, swap_block(): return lax.ppermute(block, ('row', 'col'), route)  8.7 us
  transfers between devices with their start and end apart: 4, of which 4 were waited for; matrix products, arithmetic and copies ran while one was open for 8% of the time, Pallas kernels for 0%

profile of v1, /device:TPU:1, one launch (start us, length us, event | category | flops | bytes accessed | tf_op | source)
XLA Modules:
  0.0 348.0 jit_solution(13776900160269548349)
XLA Ops:
  6.5 0.0 copy-start.5
  6.5 0.0 all-gather.2.cloned.1.call-start
  6.5 1.8 convert_element_type.70
  8.3 0.1 slice.166
  8.4 6.2 %collective-permute-start = (bf16[15,128,256]{2,1,0:T(8,128)(2,1)S(1)}, bf16[15,128,256]{2,1,0:T(8,128)(2,1)S(1)}, u32[]{:S(2)}, u32[]{:S(2)}) collective-permute-start(bf16[15,128,256]{2,1,0:T(8,128)(2,1)S(1)} %bitcast.63), channel_id=1, source_target_pairs={{0,1},{1,2},{2,3},{3,4},{4,5},{5,6},{6,7},{7,8},{8,9},{9,10},{10,1... | collective-permute-start | bytes 2949128 | tf_op jit(solution)/shard_map/ppermute | solution.py:17
  14.6 0.0 copy-done.5
  14.7 0.2 fusion.128
  14.8 10.8 %collective-permute-done = bf16[15,128,256]{2,1,0:T(8,128)(2,1)S(1)} collective-permute-done((bf16[15,128,256]{2,1,0:T(8,128)(2,1)S(1)}, bf16[15,128,256]{2,1,0:T(8,128)(2,1)S(1)}, u32[]{:S(2)}, u32[]{:S(2)}) %collective-permute-start) | collective-permute-done | bytes 983072 | tf_op jit(solution)/shard_map/ppermute | solution.py:17
  25.6 5.2 %fusion.72 = bf16[64,16,256]{2,0,1:T(8,128)(2,1)S(1)} fusion(bf16[16,128,256]{2,1,0:T(8,128)(2,1)S(1)} %bitcast.58, bf16[15,128,256]{2,1,0:T(8,128)(2,1)S(1)} %collective-permute-done, f32[128]{0:T(128)S(1)} %get-tuple-element.16, f32[128]{0:T(128)S(1)} %get-tuple-element.17, f32[128]{0:T(128)S(1)} %get-tuple-element.18, f32[128]{0:T(128)S(1)} %get-tuple-element.19, ...), kind=kOutput, calls=%fused_computation.103 | convolution fusion | flops 451420160 | bytes 2596864 | tf_op jit(solution)/shard_map/sni,nk->ksi/dot_general | solution.py:43
  30.8 0.0 copy-start.4
  30.8 1.9 collective-permute-start.1
  32.7 0.0 copy-done.4
  32.7 0.0 all-gather.2.cloned.1.call-update
  32.8 8.7 %collective-permute-done.1 = bf16[2,32,16,256]{3,1,0,2:T(8,128)(2,1)S(1)} collective-permute-done((bf16[2,32,16,256]{3,1,0,2:T(8,128)(2,1)S(1)}, bf16[2,32,16,256]{3,1,0,2:T(8,128)(2,1)S(1)}, u32[]{:S(2)}, u32[]{:S(2)}) %collective-permute-start.1) | collective-permute-done | bytes 524320 | tf_op jit(solution)/shard_map/ppermute | solution.py:23
  41.5 0.3 copy.7
  41.8 4.3 %stack.2 = bf16[16,2,32,16,256]{4,3,2,1,0:T(8,128)(2,1)} broadcast(bf16[2,32,16,256]{3,2,1,0:T(8,128)(2,1)S(1)} %copy.7), dimensions={1,2,3,4} | broadcast | bytes 8912896 | tf_op jit(solution)/shard_map/stack | solution.py:90
  46.1 49.7 %all-to-all-start = ((bf16[16,2,32,16,256]{4,3,2,1,0:T(8,128)(2,1)}), bf16[16,2,32,16,256]{4,3,2,1,0:T(8,128)(2,1)}, u32[]{:S(2)}, u32[]{:S(2)}) async-start(bf16[16,2,32,16,256]{4,3,2,1,0:T(8,128)(2,1)} %stack.2), calls=%async_computation | async-start | bytes 16777216 | tf_op jit(solution)/shard_map/all_to_all | solution.py:90
  95.8 51.0 %all-gather.2.cloned.1.call-done = bf16[2,32,256,256]{3,1,0,2:T(8,128)(2,1)} async-done(((bf16[2,32,16,256]{3,1,0,2:T(8,128)(2,1)}), bf16[2,32,256,256]{3,1,0,2:T(8,128)(2,1)}) %all-gather.2.cloned.1.call-update) | async-done | bytes 8388624 | tf_op jit(solution)/shard_map/all_gather | solution.py:88
  146.9 5.8 %fusion.135 = (bf16[1,32,128,256]{3,1,0,2:T(8,128)(2,1)}, bf16[1,32,128,256]{3,1,0,2:T(8,128)(2,1)}, bf16[1,32,128,256]{3,1,0,2:T(8,128)(2,1)}, bf16[1,32,128,256]{3,1,0,2:T(8,128)(2,1)S(1)}) fusion(bf16[2,32,256,256]{3,1,0,2:T(8,128)(2,1)} %all-gather.2.cloned.1.call-done), kind=kLoop, calls=%fused_computation.173 | loop fusion | bytes 16777216 | tf_op jit(solution)/shard_map/slice | solution.py:55
  152.6 4.5 %copy.13 = bf16[1,32,128,256]{2,3,1,0:T(8,128)(2,1)} copy(bf16[1,32,128,256]{3,1,0,2:T(8,128)(2,1)} %get-tuple-element.5) | data formatting | bytes 4194304
  157.2 4.5 %copy.12 = bf16[1,32,128,256]{2,3,1,0:T(8,128)(2,1)} copy(bf16[1,32,128,256]{3,1,0,2:T(8,128)(2,1)} %get-tuple-element.6) | data formatting | bytes 4194304
  161.7 4.5 %copy.11 = bf16[1,32,128,256]{2,3,1,0:T(8,128)(2,1)} copy(bf16[1,32,128,256]{3,1,0,2:T(8,128)(2,1)} %get-tuple-element.7) | data formatting | bytes 4194304
  166.2 3.1 copy.14
  169.3 118.1 %all-to-all-done = bf16[16,2,32,16,256]{4,3,2,1,0:T(8,128)(2,1)} async-done(((bf16[16,2,32,16,256]{4,3,2,1,0:T(8,128)(2,1)}), bf16[16,2,32,16,256]{4,3,2,1,0:T(8,128)(2,1)}, u32[]{:S(2)}, u32[]{:S(2)}) %all-to-all-start) | async-done | bytes 8388640 | tf_op jit(solution)/shard_map/all_to_all | solution.py:90
  287.4 8.0 %copy.8 = bf16[2,32,16,16,256]{4,3,2,1,0:T(8,128)(2,1)} copy(bf16[2,32,16,16,256]{4,3,1,0,2:T(8,128)(2,1)} %bitcast.22) | data formatting | bytes 16777216 | tf_op jit(solution)/shard_map/reshape | solution.py:89
  295.4 0.0 copy-start
  295.4 4.0 %fusion.134 = (bf16[32,128,256]{2,1,0:T(8,128)(2,1)}, bf16[32,128,256]{2,1,0:T(8,128)(2,1)S(1)}) fusion(bf16[2,32,256,256]{3,2,1,0:T(8,128)(2,1)} %bitcast.56), kind=kLoop, calls=%fused_computation.172 | loop fusion | flops 2097152 | bytes 8388608 | tf_op jit(solution)/shard_map/neg | solution.py:65
  299.4 1.4 copy-done
  300.8 0.0 copy-start.2
  300.8 0.0 copy-start.3
  300.8 4.2 %slice_bitcast_fusion = (bf16[32,128,256]{2,1,0:T(8,128)(2,1)}, bf16[32,128,256]{2,1,0:T(8,128)(2,1)}, bf16[32,128,256]{2,1,0:T(8,128)(2,1)}, bf16[32,128,256]{2,1,0:T(8,128)(2,1)}) fusion(bf16[2,32,256,256]{3,2,1,0:T(8,128)(2,1)S(1)} %bitcast.57), kind=kLoop, calls=%fused_computation.50 | loop fusion | bytes 16777216 | tf_op jit(solution)/shard_map/squeeze | solution.py:61
  304.9 0.0 copy-done.2
  304.9 0.8 copy-done.3
  305.8 0.0 copy-start.1
  305.8 9.2 %fusion = f32[32,256,512]{2,1,0:T(8,128)} fusion(bf16[32,128,256]{2,1,0:T(8,128)(2,1)} %get-tuple-element.12, bf16[32,128,256]{2,1,0:T(8,128)(2,1)S(1)} %get-tuple-element.14, bf16[32,128,256]{2,1,0:T(8,128)(2,1)} %get-tuple-element.11, bf16[32,128,256]{1,2,0:T(8,128)(2,1)S(1)} %bitcast.61, bf16[32,128,256]{1,2,0:T(8,128)(2,1)S(1)} %bitcast.62), kind=kOutput, calls=%fused_computation.1 | convolution fusion | flops 2189426688 | bytes 27262976 | tf_op jit(solution)/shard_map/dot_general | solution.py:69
  315.0 0.0 copy-done.1
  315.0 13.6 %multiply_convert_fusion = bf16[32,256,512]{2,1,0:T(8,128)(2,1)} fusion(f32[32,256,512]{2,1,0:T(8,128)} %fusion, bf16[32,128,256]{2,1,0:T(8,128)(2,1)} %get-tuple-element.10, bf16[32,128,256]{2,1,0:T(8,128)(2,1)} %get-tuple-element.13, bf16[32,128,256]{2,1,0:T(8,128)(2,1)} %get-tuple-element.9, bf16[32,128,256]{1,2,0:T(8,128)(2,1)} %bitcast.60, ...), kind=kOutput, calls=%fused_computation | convolution fusion | flops 2202009600 | bytes 35651584 | tf_op jit(solution)/shard_map/dot_general | solution.py:69
  328.7 12.5 %reshape.40 = bf16[32,256,2,256]{3,2,1,0:T(2,128)(2,1)} reshape(bf16[32,256,512]{2,1,0:T(8,128)(2,1)} %multiply_convert_fusion) | data formatting | bytes 16777216 | tf_op jit(solution)/shard_map/reshape | solution.py:78
  (3 shorter events, 0.0 us)
Async XLA Ops:
  6.5 8.1 %copy-start.5 = (s32[16,128]{1,0:T(8,128)S(1)}, s32[16,128]{1,0:T(8,128)}, u32[]{:S(2)}) copy-start(s32[16,128]{1,0:T(8,128)} %param.3) | copy-start | bytes 24580
  6.5 140.3 %all-gather.2.cloned.1.call-start = ((), (), s32[]{:S(2)}) async-start(), calls=%async_computation.1 | async-start | bytes 8912896 | tf_op jit(solution)/shard_map/all_gather | solution.py:88
  8.4 17.2 %collective-permute-start = (bf16[15,128,256]{2,1,0:T(8,128)(2,1)S(1)}, bf16[15,128,256]{2,1,0:T(8,128)(2,1)S(1)}, u32[]{:S(2)}, u32[]{:S(2)}) collective-permute-start(bf16[15,128,256]{2,1,0:T(8,128)(2,1)S(1)} %bitcast.63), channel_id=1, source_target_pairs={{0,1},{1,2},{2,3},{3,4},{4,5},{5,6},{6,7},{7,8},{8,9},{9,10},{10,1... | collective-permute-start | bytes 2949128 | tf_op jit(solution)/shard_map/ppermute | solution.py:17
  30.8 1.9 copy-start.4
  30.8 10.7 %collective-permute-start.1 = (bf16[2,32,16,256]{3,1,0,2:T(8,128)(2,1)S(1)}, bf16[2,32,16,256]{3,1,0,2:T(8,128)(2,1)S(1)}, u32[]{:S(2)}, u32[]{:S(2)}) collective-permute-start(bf16[2,32,16,256]{3,1,0,2:T(8,128)(2,1)S(1)} %bitcast.64), channel_id=1, source_target_pairs={{0,0},{1,16},{2,32},{3,48},{4,64},{5,80},{6,96},{7,112},{8,128},{9... | collective-permute-start | bytes 1572872 | tf_op jit(solution)/shard_map/ppermute | solution.py:23
  46.1 241.3 %all-to-all-start = ((bf16[16,2,32,16,256]{4,3,2,1,0:T(8,128)(2,1)}), bf16[16,2,32,16,256]{4,3,2,1,0:T(8,128)(2,1)}, u32[]{:S(2)}, u32[]{:S(2)}) async-start(bf16[16,2,32,16,256]{4,3,2,1,0:T(8,128)(2,1)} %stack.2), calls=%async_computation | async-start | bytes 16777216 | tf_op jit(solution)/shard_map/all_to_all | solution.py:90
  295.4 5.4 %copy-start = (bf16[2,32,16,16,256]{4,3,2,1,0:T(8,128)(2,1)S(1)}, bf16[2,32,16,16,256]{4,3,2,1,0:T(8,128)(2,1)}, u32[]{:S(2)}) copy-start(bf16[2,32,16,16,256]{4,3,2,1,0:T(8,128)(2,1)} %copy.8) | copy-start | bytes 25165828
  300.8 4.2 %copy-start.2 = (bf16[1,32,128,256]{2,3,1,0:T(8,128)(2,1)S(1)}, bf16[1,32,128,256]{2,3,1,0:T(8,128)(2,1)}, u32[]{:S(2)}) copy-start(bf16[1,32,128,256]{2,3,1,0:T(8,128)(2,1)} %copy.12) | copy-start | bytes 6291460
  300.8 5.0 %copy-start.3 = (bf16[1,32,128,256]{2,3,1,0:T(8,128)(2,1)S(1)}, bf16[1,32,128,256]{2,3,1,0:T(8,128)(2,1)}, u32[]{:S(2)}) copy-start(bf16[1,32,128,256]{2,3,1,0:T(8,128)(2,1)} %copy.11) | copy-start | bytes 6291460
  305.8 9.2 %copy-start.1 = (bf16[1,32,128,256]{2,3,1,0:T(8,128)(2,1)S(1)}, bf16[1,32,128,256]{2,3,1,0:T(8,128)(2,1)}, u32[]{:S(2)}) copy-start(bf16[1,32,128,256]{2,3,1,0:T(8,128)(2,1)} %copy.13) | copy-start | bytes 6291460
Sparse Core Ops, SparseCore 0:
  32.9 113.9 all-gather.1
